TPU v7x, 256 devices: a whole 4x4x8 slice. The times are simulated.
256 devices in a mesh: dp: 8 (over z_hi, x), expert: 32 (over z_lo, y, core).
Axes of the slice: x: 4, y: 4, z: 8 (z_hi: 2, z_lo: 4; z = z_hi * 4 + z_lo), core: 2. Of those that a mesh axis runs over, the one named last changes fastest.
Arguments:
- tokens: bfloat16 [32768, 3584], P(('dp', 'expert')), may hold values from -6 to 6
- cotangent: bfloat16 [32768, 3584], P(('dp', 'expert')), may hold values from -0.09375 to 0.09375
- expert_ids: int32 [32768, 8], P(('dp', 'expert')), may hold values from 0 to 255, all different within a row; in each aligned block of 128 rows (0 to 127, 128 to 255, ...) at most 6 rows name the same one
- gates: bfloat16 [32768, 8], P(('dp', 'expert')), may hold values from 0.049804688 to 1
- swap_flags: int32 [16], replicated, may hold values 0 or 1
- gate_w: bfloat16 [32, 3584, 1024], P('expert', None, 'dp'), may hold values from -0.09375 to 0.09375
- up_w: bfloat16 [32, 3584, 1024], P('expert', None, 'dp'), may hold values from -0.09375 to 0.09375
- down_w: bfloat16 [32, 1024, 3584], P('expert', 'dp'), may hold values from -0.1875 to 0.1875
Outputs:
- grad_gate_w: bfloat16 [32, 3584, 1024], P('expert', None, 'dp')
- grad_up_w: bfloat16 [32, 3584, 1024], P('expert', None, 'dp')
- grad_down_w: bfloat16 [32, 1024, 3584], P('expert', 'dp')
- score_grad: float32 [32768, 8], P(('dp', 'expert'))
Inputs may be any that keep to these rules, and one draw needn't show every extreme that they name: `expert_ids`: among the 128 rows of one device no expert is named more than 6 times, a bound that some block reaches; the numbers of one row differ. `swap_flags`: 1 means that slots s and s + 16 trade their experts.
All inputs are finite; a program needn't handle non-finite values.
Results may differ from a plain program's by a relative error of at most 0.011.
Values may be sent and summed in bfloat16 or wider, within the bound.
A program may use at most 128 MiB of HBM per device.

v0:
```python
import jax
import jax.numpy as jnp
from jax import lax
from jax.sharding import PartitionSpec as P

CAP = 6


def partner(block, axis, stride):
    count = lax.axis_size(axis)
    route = []
    for low in range(count):
        high = low | 1 << stride
        if high != low and high < count:
            route += [(low, high), (high, low)]
    return lax.ppermute(block, axis, route)


def body(tokens, cotangent, expert_ids, gates, swap_flags, gate_w, up_w, down_w):
    axis_len = lax.axis_size("expert")
    half_axis = axis_len // 2
    pair_bit = axis_len.bit_length() - 2
    own_slot = lax.axis_index("expert")
    tok_count = tokens.shape[0]
    top_count = expert_ids.shape[1]
    width = tokens.shape[1]
    flat_ids = expert_ids.reshape(-1)
    choice_count = flat_ids.shape[0]
    valid = flat_ids < axis_len
    pair_index = jnp.arange(half_axis, dtype=jnp.int32)
    flag_of = jnp.sum(
        jnp.where((flat_ids % half_axis)[:, None] == pair_index[None, :], swap_flags[None, :], 0),
        axis=1,
    )
    own_flag = jnp.sum(jnp.where(pair_index == own_slot % half_axis, swap_flags, 0))
    target = jnp.where(flag_of == 1, jnp.bitwise_xor(flat_ids, half_axis), flat_ids)
    target = jnp.where(valid, target, 0)
    onehot = jnp.where(
        (target[:, None] == jnp.arange(axis_len, dtype=jnp.int32)[None, :]) & valid[:, None], 1, 0
    ).astype(jnp.int32)
    ranks = jnp.sum(jnp.cumsum(onehot, axis=0) * onehot, axis=1) - 1
    slot_count = axis_len * CAP
    slots = jnp.where(valid, target * CAP + ranks, slot_count)
    source = (
        jnp.full((slot_count,), choice_count, jnp.int32)
        .at[slots]
        .set(jnp.arange(choice_count, dtype=jnp.int32), mode="drop")
    )
    token_index = source // top_count
    padded_x = jnp.concatenate([tokens, jnp.zeros((1, width), tokens.dtype)], axis=0)
    padded_dy = jnp.concatenate([cotangent, jnp.zeros((1, width), cotangent.dtype)], axis=0)
    padded_g = jnp.concatenate([gates.reshape(-1), jnp.zeros((1,), gates.dtype)], axis=0)
    send_x = padded_x[token_index].reshape(axis_len, CAP, width)
    send_dy = padded_dy[token_index].reshape(axis_len, CAP, width)
    send_g = padded_g[source].reshape(axis_len, CAP)
    recv_x, recv_dy, recv_g = (
        lax.all_to_all(send_x, "expert", split_axis=0, concat_axis=0, tiled=True),
        lax.all_to_all(send_dy, "expert", split_axis=0, concat_axis=0, tiled=True),
        lax.all_to_all(send_g, "expert", split_axis=0, concat_axis=0, tiled=True),
    )
    w_gate = gate_w[0]
    w_up = up_w[0]
    w_down = down_w[0]
    other_gate, other_up, other_down = partner((gate_w, up_w, down_w), "expert", pair_bit)
    taken = own_flag == 1
    w_gate = jnp.where(taken, other_gate[0], w_gate)
    w_up = jnp.where(taken, other_up[0], w_up)
    w_down = jnp.where(taken, other_down[0], w_down)
    contract = (((0,), (0,)), ((), ()))
    part_x = lax.all_gather(recv_x, "dp", axis=0, tiled=True)
    part_dy = lax.all_gather(recv_dy, "dp", axis=0, tiled=True)
    part_g = lax.all_gather(recv_g, "dp", axis=0, tiled=True)
    block_count = part_x.shape[0]
    row_x = part_x.reshape(-1, width)
    row_dy = part_dy.reshape(-1, width)
    row_g = part_g.reshape(-1, 1)
    pre_gate = jnp.dot(row_x, w_gate, preferred_element_type=jnp.float32)
    pre_up = jnp.dot(row_x, w_up, preferred_element_type=jnp.float32)
    sigma = jax.nn.sigmoid(pre_gate)
    active = pre_gate * sigma
    hidden = (active * pre_up).astype(jnp.bfloat16)
    back = lax.dot_general(
        row_dy, w_down, (((1,), (1,)), ((), ())), preferred_element_type=jnp.float32
    )
    score = jnp.sum(hidden.astype(jnp.float32) * back, axis=1)
    scaled = row_dy * row_g
    d_hidden = row_g.astype(jnp.float32) * back
    d_gate = (d_hidden * pre_up * sigma * (1.0 + pre_gate * (1.0 - sigma))).astype(jnp.bfloat16)
    d_up = (d_hidden * active).astype(jnp.bfloat16)
    grad_gate = lax.dot_general(row_x, d_gate, contract, preferred_element_type=jnp.float32)
    grad_up = lax.dot_general(row_x, d_up, contract, preferred_element_type=jnp.float32)
    grad_down = lax.dot_general(hidden, scaled, contract, preferred_element_type=jnp.float32)
    scores = score.reshape(block_count, CAP)
    grad_gate, grad_up, grad_down, scores = (grad_gate, grad_up, grad_down, scores)
    summed = lax.psum(scores, "dp")
    own_scores = lax.dynamic_slice_in_dim(summed, lax.axis_index("dp") * axis_len, axis_len, 0)
    returned = lax.all_to_all(own_scores, "expert", split_axis=0, concat_axis=0, tiled=True)
    picked = returned.reshape(-1)[jnp.minimum(slots, slot_count - 1)]
    score_grad = jnp.where(valid, picked, 0.0).reshape(tok_count, top_count)
    out_gate = grad_gate.astype(jnp.bfloat16)[None]
    out_up = grad_up.astype(jnp.bfloat16)[None]
    out_down = grad_down.astype(jnp.bfloat16)[None]
    return (out_gate, out_up, out_down, score_grad)


def solution(mesh):
    placed = (
        P(("dp", "expert"), None),
        P(("dp", "expert"), None),
        P(("dp", "expert"), None),
        P(("dp", "expert"), None),
        P(),
        P("expert", None, "dp"),
        P("expert", None, "dp"),
        P("expert", "dp", None),
    )
    return jax.shard_map(
        body,
        mesh=mesh,
        in_specs=placed,
        out_specs=(
            P("expert", None, "dp"),
            P("expert", None, "dp"),
            P("expert", "dp", None),
            P(("dp", "expert"), None),
        ),
        check_vma=False,
    )
```

profile of v0, /device:TPU:1, one launch (start us, length us, event | category | flops | bytes accessed | tf_op | source)
XLA Modules:
  0.0 742.2 jit_solution(1144176695480367231)
XLA Ops:
  7.2 0.8 copy.63
  9.1 9.0 %reduce-window.6 = s32[32,8,128]{2,1,0:T(8,128)S(1)} reduce-window(s32[32,8,128]{2,1,0:T(8,128)S(1)} %fusion.31, s32[]{:T(128)} %constant.32.clone.1), window={size=1x1x128 pad=0_0x0_0x127_0}, to_apply=%region_1.2 | reduce-window | flops 4161536 | bytes 262148 | tf_op jit(solution)/shard_map/reduce-window
  18.7 4.3 scatter_custom_fusion
  23.1 1.2 concatenate.9
  24.3 1.4 gather_fusion
  26.2 54.0 %all_to_all.32 = bf16[32,6,3584]{2,1,0:T(8,128)(2,1)S(1)} all-to-all(bf16[32,6,3584]{2,1,0:T(8,128)(2,1)S(1)} %reshape.224), channel_id=1, replica_groups=mesh['dp'=8,'expert'=32] {'expert'}, dimensions={0} | all-to-all | bytes 2752512 | tf_op jit(solution)/shard_map/all_to_all | solution.py:57
  80.2 1.5 copy.68
  81.8 1.2 concatenate.11
  83.1 1.4 gather_fusion.2
  85.0 78.0 %all_to_all.33 = bf16[32,6,3584]{2,1,0:T(8,128)(2,1)S(1)} all-to-all(bf16[32,6,3584]{2,1,0:T(8,128)(2,1)S(1)} %reshape.228), channel_id=1, replica_groups=mesh['dp'=8,'expert'=32] {'expert'}, dimensions={0} | all-to-all | bytes 2752512 | tf_op jit(solution)/shard_map/all_to_all | solution.py:58
  163.0 1.6 copy.72
  164.5 1.0 collective-permute-start.1
  165.5 1.5 collective-permute-start.2
  167.0 0.9 collective-permute-start
  168.1 1.6 gather_fusion.1
  170.5 5.8 all-to-all-start.1
  177.6 242.5 %all-to-all-done.1 = bf16[32,1,6]{2,1,0:T(2,128)(2,1)S(1)} async-done(((bf16[32,1,6]{2,1,0:T(2,128)(2,1)}), bf16[32,1,6]{2,1,0:T(2,128)(2,1)S(1)}, u32[]{:S(2)}, u32[]{:S(2)}) %all-to-all-start.1) | async-done | bytes 416 | tf_op jit(solution)/shard_map/all_to_all | solution.py:59
  420.1 43.9 %all-gather = bf16[256,1,6]{2,1,0:T(2,128)(2,1)S(1)} all-gather(bf16[32,1,6]{2,1,0:T(2,128)(2,1)S(1)} %all-to-all-done.1), channel_id=2, replica_groups=mesh['dp'=8,'expert'=32] {'dp'}, dimensions={0}, use_global_device_ids=true | all-gather | bytes 3456 | tf_op jit(solution)/shard_map/all_gather | solution.py:72
  464.5 13.1 %copy.69 = bf16[256,6,3584]{2,1,0:T(8,128)(2,1)} copy(bf16[256,6,3584]{2,0,1:T(8,128)(2,1)} %all-gather.4.cloned.1.call-done) | data formatting | bytes 22020096 | tf_op jit(solution)/shard_map/all_gather | solution.py:70
  477.6 17.7 %reshape.225 = bf16[1536,3584]{1,0:T(8,128)(2,1)} reshape(bf16[256,6,3584]{2,1,0:T(8,128)(2,1)} %copy.69) | data formatting | bytes 22020096 | tf_op jit(solution)/shard_map/reshape | solution.py:74
  495.3 106.1 %all-gather.6.cloned.1.call-done = bf16[256,6,3584]{2,0,1:T(8,128)(2,1)} async-done(((bf16[32,6,3584]{2,0,1:T(8,128)(2,1)}), bf16[256,6,3584]{2,0,1:T(8,128)(2,1)}) %all-gather.6.cloned.1.call-update) | async-done | bytes 11010064 | tf_op jit(solution)/shard_map/all_gather | solution.py:71
  601.5 13.1 %copy.73 = bf16[256,6,3584]{2,1,0:T(8,128)(2,1)} copy(bf16[256,6,3584]{2,0,1:T(8,128)(2,1)} %all-gather.6.cloned.1.call-done) | data formatting | bytes 22020096 | tf_op jit(solution)/shard_map/all_gather | solution.py:71
  614.5 17.8 %reshape.229 = bf16[1536,3584]{1,0:T(8,128)(2,1)} reshape(bf16[256,6,3584]{2,1,0:T(8,128)(2,1)} %copy.73) | data formatting | bytes 22020096 | tf_op jit(solution)/shard_map/reshape | solution.py:75
  632.4 8.0 %fusion.13 = f32[1536,128]{0,1:T(8,128)S(1)} fusion(bf16[1536,3584]{1,0:T(8,128)(2,1)} %reshape.225, bf16[1,3584,128]{2,1,0:T(8,128)(2,1)S(1)} %collective-permute-done.1, bf16[1,3584,128]{2,1,0:T(8,128)(2,1)S(1)} %copy-done, pred[]{:T(512)S(6)} %eq.85), kind=kOutput, calls=%fused_computation.16 | convolution fusion | flops 1409744896 | bytes 13631489 | tf_op jit(solution)/shard_map/dot_general | solution.py:78
  640.4 8.2 %fusion.11 = f32[1536,128]{0,1:T(8,128)S(1)} fusion(bf16[1536,3584]{1,0:T(8,128)(2,1)} %reshape.225, bf16[1,3584,128]{2,1,0:T(8,128)(2,1)} %collective-permute-done.2, bf16[1,3584,128]{2,1,0:T(8,128)(2,1)} %param.13, pred[]{:T(512)S(6)} %eq.85), kind=kOutput, calls=%fused_computation.14 | convolution fusion | flops 1409744896 | bytes 13631489 | tf_op jit(solution)/shard_map/dot_general | solution.py:77
  648.7 5.7 multiply_reduce_fusion
  654.4 4.0 fusion.7
  658.4 4.3 fusion.6
  662.9 41.4 %psum.7 = f32[256,6]{1,0:T(8,128)S(1)} all-reduce(f32[256,6]{1,0:T(8,128)S(1)} %reshape.230), channel_id=1, replica_groups=mesh['dp'=8,'expert'=32] {'dp'}, use_global_device_ids=true, to_apply=%region_7.8 | all-reduce | flops 1536 | bytes 12288 | tf_op jit(solution)/shard_map/psum | solution.py:95
  704.8 14.3 %all-to-all-start.3 = ((f32[32,1,6]{2,1,0:T(1,128)}), f32[32,1,6]{2,1,0:T(1,128)S(1)}, u32[]{:S(2)}, u32[]{:S(2)}) async-start(f32[32,1,6]{2,1,0:T(1,128)} %bitcast.11), calls=%async_computation.3 | async-start | bytes 32768 | tf_op jit(solution)/shard_map/all_to_all | solution.py:97
  719.2 6.9 fusion.8
  727.8 6.8 gather_fusion.3
  (75 shorter events, 8.2 us)
Async XLA Ops:
  7.2 457.4 %all-gather.4.cloned.1.call-start = ((), (), s32[]{:S(2)}) async-start(), calls=%async_computation.4 | async-start | bytes 12386304 | tf_op jit(solution)/shard_map/all_gather | solution.py:70
  81.7 519.7 %all-gather.6.cloned.1.call-start = ((), (), s32[]{:S(2)}) async-start(), calls=%async_computation.5 | async-start | bytes 12386304 | tf_op jit(solution)/shard_map/all_gather | solution.py:71
  83.0 84.8 %copy-start.2 = (bf16[128,8]{0,1:T(8,128)(2,1)S(1)}, bf16[128,8]{0,1:T(8,128)(2,1)}, u32[]{:S(2)}) copy-start(bf16[128,8]{0,1:T(8,128)(2,1)} %param.11) | copy-start | bytes 6148
  83.1 93.3 %copy-start.3 = (s32[16]{0:T(128)S(1)}, s32[16]{0:T(128)}, u32[]{:S(2)}) copy-start(s32[16]{0:T(128)} %param.12) | copy-start | bytes 196
  164.5 467.8 %collective-permute-start.1 = (bf16[1,3584,128]{2,1,0:T(8,128)(2,1)}, bf16[1,3584,128]{2,1,0:T(8,128)(2,1)S(1)}, u32[]{:S(2)}, u32[]{:S(2)}) collective-permute-start(bf16[1,3584,128]{2,1,0:T(8,128)(2,1)} %param.14), channel_id=1, source_target_pairs={{0,16},{16,0},{1,17},{17,1},{2,18},{18,2},{3,19},{19,3},{4,20},{20... | collective-permute-start | bytes 2752520 | tf_op jit(solution)/shard_map/ppermute | solution.py:16
  165.5 474.9 %collective-permute-start.2 = (bf16[1,3584,128]{2,1,0:T(8,128)(2,1)}, bf16[1,3584,128]{2,1,0:T(8,128)(2,1)}, u32[]{:S(2)}, u32[]{:S(2)}) collective-permute-start(bf16[1,3584,128]{2,1,0:T(8,128)(2,1)} %param.13), channel_id=1, source_target_pairs={{0,16},{16,0},{1,17},{17,1},{2,18},{18,2},{3,19},{19,3},{4,20},{20... | collective-permute-start | bytes 2752520 | tf_op jit(solution)/shard_map/ppermute | solution.py:16
  167.0 481.6 %collective-permute-start = (bf16[1,128,3584]{2,1,0:T(8,128)(2,1)}, bf16[1,128,3584]{2,1,0:T(8,128)(2,1)}, u32[]{:S(2)}, u32[]{:S(2)}) collective-permute-start(bf16[1,128,3584]{2,1,0:T(8,128)(2,1)} %param.15), channel_id=1, source_target_pairs={{0,16},{16,0},{1,17},{17,1},{2,18},{18,2},{3,19},{19,3},{4,20},{20... | collective-permute-start | bytes 2752520 | tf_op jit(solution)/shard_map/ppermute | solution.py:16
  170.5 249.6 %all-to-all-start.1 = ((bf16[32,1,6]{2,1,0:T(2,128)(2,1)}), bf16[32,1,6]{2,1,0:T(2,128)(2,1)S(1)}, u32[]{:S(2)}, u32[]{:S(2)}) async-start(bf16[32,1,6]{2,1,0:T(2,128)(2,1)} %all_to_all.27), calls=%async_computation.1 | async-start | bytes 32768 | tf_op jit(solution)/shard_map/all_to_all | solution.py:59
  614.5 17.8 %copy-start = (bf16[1,3584,128]{2,1,0:T(8,128)(2,1)S(1)}, bf16[1,3584,128]{2,1,0:T(8,128)(2,1)}, u32[]{:S(2)}) copy-start(bf16[1,3584,128]{2,1,0:T(8,128)(2,1)} %param.14) | copy-start | bytes 2752516
  632.3 16.3 %slice-start.3 = ((s8[11010048]{0:T(1024)(128)(4,1)}), s8[4194304]{0:T(1024)(128)(4,1)S(1)}, s32[]{:S(2)}) async-start(s8[11010048]{0:T(1024)(128)(4,1)} %bitcast.45), calls=%async_computation.9 | async-start | bytes 8388608
  632.3 16.3 %slice-start.4 = ((s8[11010048]{0:T(1024)(128)(4,1)}), s8[4194304]{0:T(1024)(128)(4,1)S(1)}, s32[]{:S(2)}) async-start(s8[11010048]{0:T(1024)(128)(4,1)} %bitcast.45), calls=%async_computation.10 | async-start | bytes 8388608
  640.4 8.3 %slice-start.5 = ((s8[11010048]{0:T(1024)(128)(4,1)}), s8[2621440]{0:T(1024)(128)(4,1)S(1)}, s32[]{:S(2)}) async-start(s8[11010048]{0:T(1024)(128)(4,1)} %bitcast.45), calls=%async_computation.11 | async-start | bytes 5242880
  640.4 14.0 %slice-start = ((s8[11010048]{0:T(1024)(128)(4,1)}), s8[4194304]{0:T(1024)(128)(4,1)S(1)}, s32[]{:S(2)}) async-start(s8[11010048]{0:T(1024)(128)(4,1)} %bitcast.43), calls=%async_computation.6 | async-start | bytes 8388608
  640.4 14.0 %slice-start.1 = ((s8[11010048]{0:T(1024)(128)(4,1)}), s8[2621440]{0:T(1024)(128)(4,1)S(1)}, s32[]{:S(2)}) async-start(s8[11010048]{0:T(1024)(128)(4,1)} %bitcast.43), calls=%async_computation.7 | async-start | bytes 5242880
  648.6 5.8 slice-start.2
  658.4 60.7 %copy-start.4 = (bf16[1536,128]{0,1:T(8,128)(2,1)S(1)}, bf16[1536,128]{0,1:T(8,128)(2,1)}, u32[]{:S(2)}) copy-start(bf16[1536,128]{0,1:T(8,128)(2,1)} %get-tuple-element.23) | copy-start | bytes 1179652
  662.7 72.1 %copy-start.1 = (s32[128,8]{0,1:T(8,128)S(1)}, s32[128,8]{0,1:T(8,128)}, u32[]{:S(2)}) copy-start(s32[128,8]{0,1:T(8,128)} %param.10) | copy-start | bytes 12292
  704.8 21.6 %all-to-all-start.3 = ((f32[32,1,6]{2,1,0:T(1,128)}), f32[32,1,6]{2,1,0:T(1,128)S(1)}, u32[]{:S(2)}, u32[]{:S(2)}) async-start(f32[32,1,6]{2,1,0:T(1,128)} %bitcast.11), calls=%async_computation.3 | async-start | bytes 32768 | tf_op jit(solution)/shard_map/all_to_all | solution.py:97
Sparse Core Ops, SparseCore 0:
  81.9 288.9 all-gather.3
  373.4 228.0 all-gather.5
where the time goes:
time: 744 us; the launch traced here: 742 us
  waiting for transfers between devices  349 us (47%)
  blocking collectives  217 us (29%)
  local copies, waits for them, and re-layouts  87.8 us (12%)
  matrix products  37.1 us (5%)
  starting transfers between devices  23.6 us (3%)
  between operations  15.1 us (2%)
  other arithmetic  12.4 us (2%)
    all_to_all x1, waiting for transfers between devices, body(): lax.all_to_all(send_g, 'expert', split_axis=0, concat_axis=0, tiled=True)  242 us
    all_gather x1, waiting for transfers between devices, body(): part_dy = lax.all_gather(recv_dy, 'dp', axis=0, tiled=True)  106 us
    all_to_all x1, blocking collectives, body(): lax.all_to_all(send_dy, 'expert', split_axis=0, concat_axis=0, tiled=True)  78 us
    all_to_all x1, blocking collectives, body(): lax.all_to_all(send_x, 'expert', split_axis=0, concat_axis=0, tiled=True)  54 us
    all_gather x1, blocking collectives, body(): part_g = lax.all_gather(recv_g, 'dp', axis=0, tiled=True)  43.9 us
    psum x1, blocking collectives, body(): summed = lax.psum(scores, 'dp')  41.4 us
    reshape x1, local copies, waits for them, and re-layouts, body(): row_dy = part_dy.reshape(-1, width)  17.8 us
    reshape x1, local copies, waits for them, and re-layouts, body(): row_x = part_x.reshape(-1, width)  17.7 us
  transfers between devices with their start and end apart: 7, of which 3 were waited for; matrix products, arithmetic and copies ran while one was open for 12% of the time, Pallas kernels for 0%

commit v1 on v0

--- a/solution.py
+++ b/solution.py
@@ -67,8 +67,11 @@
     w_up = jnp.where(taken, other_up[0], w_up)
     w_down = jnp.where(taken, other_down[0], w_down)
     contract = (((0,), (0,)), ((), ()))
-    part_x = lax.all_gather(recv_x, "dp", axis=0, tiled=True)
-    part_dy = lax.all_gather(recv_dy, "dp", axis=0, tiled=True)
+    part_x, part_dy = jnp.split(
+        lax.all_gather(jnp.concatenate([recv_x, recv_dy], axis=1), "dp", axis=0, tiled=True),
+        [recv_x.shape[1]],
+        axis=1,
+    )
     part_g = lax.all_gather(recv_g, "dp", axis=0, tiled=True)
     block_count = part_x.shape[0]
     row_x = part_x.reshape(-1, width)

time: 744 us -> 778 us (1.046)
  starting transfers between devices: 23.6 us -> 66.7 us
  waiting for transfers between devices: 349 us -> 323 us
  local copies, waits for them, and re-layouts: 87.8 us -> 102 us
    all_gather x2 -> x1, waiting for transfers between devices: 106 us -> 0.02 us  [body(): lax.all_gather(jnp.concatenate([recv_x, recv_dy], axis=1), 'dp', axis=0,...]
    all_gather x1, blocking collectives: 43.9 us -> 123 us  [body(): part_g = lax.all_gather(recv_g, 'dp', axis=0, tiled=True)]
    all_to_all x1 -> x0, blocking collectives: 54 us -> none  [body(): lax.all_to_all(send_x, 'expert', split_axis=0, concat_axis=0, tiled=True)]
    all_to_all x1, waiting for transfers between devices: 242 us -> 288 us  [body(): lax.all_to_all(send_g, 'expert', split_axis=0, concat_axis=0, tiled=True)]
    all_to_all x0 -> x1, waiting for transfers between devices: none -> 35.2 us  [body(): lax.all_to_all(send_x, 'expert', split_axis=0, concat_axis=0, tiled=True)]
    split x0 -> x3, local copies, waits for them, and re-layouts: none -> 35.2 us  [body(): jnp.split(lax.all_gather(jnp.concatenate([recv_x, recv_dy], axis=1), 'dp'...]
    all_to_all x1, starting transfers between devices: 14.3 us -> 47.3 us  [body(): lax.all_to_all(own_scores, 'expert', split_axis=0, concat_axis=0, tiled=T...]
    all_to_all x1, blocking collectives: 78 us -> 50.3 us  [body(): lax.all_to_all(send_dy, 'expert', split_axis=0, concat_axis=0, tiled=True)]
  transfers between devices with their start and end apart: 7 -> 7, of which waited for: 3 -> 3; matrix products, arithmetic and copies ran while one was open for 12% -> 13% of each run, Pallas kernels for 0% -> 0%
where the time goes in v1:
time: 778 us; the launch traced here: 776 us
  waiting for transfers between devices  323 us (42%)
  blocking collectives  218 us (28%)
  local copies, waits for them, and re-layouts  102 us (13%)
  starting transfers between devices  66.7 us (9%)
  matrix products  37.2 us (5%)
  between operations  15.1 us (2%)
  other arithmetic  13.6 us (2%)
    all_to_all x1, waiting for transfers between devices, body(): lax.all_to_all(send_g, 'expert', split_axis=0, concat_axis=0, tiled=True)  288 us
    all_gather x1, blocking collectives, body(): part_g = lax.all_gather(recv_g, 'dp', axis=0, tiled=True)  123 us
    all_to_all x1, blocking collectives, body(): lax.all_to_all(send_dy, 'expert', split_axis=0, concat_axis=0, tiled=True)  50.3 us
    all_to_all x1, starting transfers between devices, body(): lax.all_to_all(own_scores, 'expert', split_axis=0, concat_axis=0, tiled=T...  47.3 us
    psum x1, blocking collectives, body(): summed = lax.psum(scores, 'dp')  44.8 us
    all_to_all x1, waiting for transfers between devices, body(): lax.all_to_all(send_x, 'expert', split_axis=0, concat_axis=0, tiled=True)  35.2 us
    split x3, local copies, waits for them, and re-layouts, body(): jnp.split(lax.all_gather(jnp.concatenate([recv_x, recv_dy], axis=1), 'dp'...  35.2 us
    reshape x1, local copies, waits for them, and re-layouts, body(): row_x = part_x.reshape(-1, width)  17.7 us
  transfers between devices with their start and end apart: 7, of which 3 were waited for; matrix products, arithmetic and copies ran while one was open for 13% of the time, Pallas kernels for 0%

profile of v1, /device:TPU:1, one launch (start us, length us, event | category | flops | bytes accessed | tf_op | source)
XLA Modules:
  0.0 776.1 jit_solution(10099934362769380648)
XLA Ops:
  9.1 9.0 %reduce-window.6 = s32[32,8,128]{2,1,0:T(8,128)S(1)} reduce-window(s32[32,8,128]{2,1,0:T(8,128)S(1)} %fusion.31, s32[]{:T(128)} %constant.32.clone.1), window={size=1x1x128 pad=0_0x0_0x127_0}, to_apply=%region_1.2 | reduce-window | flops 4161536 | bytes 262148 | tf_op jit(solution)/shard_map/reduce-window
  18.7 4.3 scatter_custom_fusion
  23.0 1.2 concatenate.12
  24.3 1.4 gather_fusion
  25.7 1.5 reshape.224
  27.2 10.2 %all-to-all-start = ((bf16[32,6,3584]{2,1,0:T(8,128)(2,1)}), bf16[32,6,3584]{2,1,0:T(8,128)(2,1)S(1)}, u32[]{:S(2)}, u32[]{:S(2)}) async-start(bf16[32,6,3584]{2,1,0:T(8,128)(2,1)} %reshape.224), calls=%async_computation | async-start | bytes 3670016 | tf_op jit(solution)/shard_map/all_to_all | solution.py:57
  37.4 1.2 concatenate.13
  38.7 2.5 gather_fusion.1
  41.2 3.4 reshape.225
  44.7 35.2 %all-to-all-done = bf16[32,6,3584]{2,1,0:T(8,128)(2,1)S(1)} async-done(((bf16[32,6,3584]{2,1,0:T(8,128)(2,1)}), bf16[32,6,3584]{2,1,0:T(8,128)(2,1)S(1)}, u32[]{:S(2)}, u32[]{:S(2)}) %all-to-all-start) | async-done | bytes 1376288 | tf_op jit(solution)/shard_map/all_to_all | solution.py:57
  79.9 50.3 %all_to_all.32 = bf16[32,6,3584]{2,1,0:T(8,128)(2,1)S(1)} all-to-all(bf16[32,6,3584]{2,1,0:T(8,128)(2,1)} %reshape.225), channel_id=1, replica_groups=mesh['dp'=8,'expert'=32] {'expert'}, dimensions={0} | all-to-all | bytes 2752512 | tf_op jit(solution)/shard_map/all_to_all | solution.py:58
  130.2 1.2 pad_maximum_fusion
  131.4 3.0 copy.65
  135.4 1.5 collective-permute-start.2
  138.0 1.6 gather_fusion.2
  140.4 5.8 all-to-all-start.2
  147.5 287.8 %all-to-all-done.2 = bf16[32,1,6]{2,1,0:T(2,128)(2,1)S(1)} async-done(((bf16[32,1,6]{2,1,0:T(2,128)(2,1)}), bf16[32,1,6]{2,1,0:T(2,128)(2,1)S(1)}, u32[]{:S(2)}, u32[]{:S(2)}) %all-to-all-start.2) | async-done | bytes 416 | tf_op jit(solution)/shard_map/all_to_all | solution.py:59
  435.3 123.2 %all-gather = bf16[256,1,6]{2,1,0:T(2,128)(2,1)S(1)} all-gather(bf16[32,1,6]{2,1,0:T(2,128)(2,1)S(1)} %all-to-all-done.2), channel_id=2, replica_groups=mesh['dp'=8,'expert'=32] {'dp'}, dimensions={0}, use_global_device_ids=true | all-gather | bytes 3456 | tf_op jit(solution)/shard_map/all_gather | solution.py:75
  559.1 12.0 %fusion.41 = (bf16[256,6,3584]{2,0,1:T(8,128)(2,1)}, bf16[256,6,3584]{2,0,1:T(8,128)(2,1)S(1)}) fusion(bf16[256,12,3584]{2,0,1:T(8,128)(2,1)} %all-gather.3.cloned.1.call-done), kind=kLoop, calls=%fused_computation.82 | loop fusion | bytes 44040192 | tf_op jit(solution)/shard_map/split | solution.py:70
  571.1 10.1 %copy.66 = bf16[256,6,3584]{2,1,0:T(8,128)(2,1)} copy(bf16[256,6,3584]{2,0,1:T(8,128)(2,1)S(1)} %get-tuple-element.27) | data formatting | bytes 22020096 | tf_op jit(solution)/shard_map/split | solution.py:70
  581.2 17.7 %reshape.226 = bf16[1536,3584]{1,0:T(8,128)(2,1)} reshape(bf16[256,6,3584]{2,1,0:T(8,128)(2,1)} %copy.66) | data formatting | bytes 22020096 | tf_op jit(solution)/shard_map/reshape | solution.py:77
  599.0 13.1 %copy.69 = bf16[256,6,3584]{2,1,0:T(8,128)(2,1)} copy(bf16[256,6,3584]{2,0,1:T(8,128)(2,1)} %get-tuple-element.26) | data formatting | bytes 22020096 | tf_op jit(solution)/shard_map/split | solution.py:70
  612.0 17.7 %reshape.229 = bf16[1536,3584]{1,0:T(8,128)(2,1)} reshape(bf16[256,6,3584]{2,1,0:T(8,128)(2,1)} %copy.69) | data formatting | bytes 22020096 | tf_op jit(solution)/shard_map/reshape | solution.py:78
  629.8 8.0 %fusion.13 = f32[1536,128]{0,1:T(8,128)S(1)} fusion(bf16[1536,3584]{1,0:T(8,128)(2,1)} %reshape.226, bf16[1,3584,128]{2,1,0:T(8,128)(2,1)S(1)} %collective-permute-done.1, bf16[1,3584,128]{2,1,0:T(8,128)(2,1)S(1)} %copy-done, pred[]{:T(512)S(6)} %eq.85), kind=kOutput, calls=%fused_computation.17 | convolution fusion | flops 1409744896 | bytes 13631489 | tf_op jit(solution)/shard_map/dot_general | solution.py:81
  637.9 8.2 %fusion.11 = f32[1536,128]{0,1:T(8,128)S(1)} fusion(bf16[1536,3584]{1,0:T(8,128)(2,1)} %reshape.226, bf16[1,3584,128]{2,1,0:T(8,128)(2,1)} %collective-permute-done.2, bf16[1,3584,128]{2,1,0:T(8,128)(2,1)} %param.13, pred[]{:T(512)S(6)} %eq.85), kind=kOutput, calls=%fused_computation.15 | convolution fusion | flops 1409744896 | bytes 13631489 | tf_op jit(solution)/shard_map/dot_general | solution.py:80
  646.1 5.7 multiply_reduce_fusion
  651.8 4.0 fusion.7
  655.9 4.3 fusion.6
  660.3 44.8 %psum.7 = f32[256,6]{1,0:T(8,128)S(1)} all-reduce(f32[256,6]{1,0:T(8,128)S(1)} %reshape.230), channel_id=1, replica_groups=mesh['dp'=8,'expert'=32] {'dp'}, use_global_device_ids=true, to_apply=%region_7.8 | all-reduce | flops 1536 | bytes 12288 | tf_op jit(solution)/shard_map/psum | solution.py:98
  705.7 47.3 %all-to-all-start.3 = ((f32[32,1,6]{2,1,0:T(1,128)}), f32[32,1,6]{2,1,0:T(1,128)S(1)}, u32[]{:S(2)}, u32[]{:S(2)}) async-start(f32[32,1,6]{2,1,0:T(1,128)} %bitcast.11), calls=%async_computation.3 | async-start | bytes 32768 | tf_op jit(solution)/shard_map/all_to_all | solution.py:100
  753.1 6.9 fusion.8
  761.7 6.8 gather_fusion.3
  (74 shorter events, 9.8 us)
Async XLA Ops:
  27.2 52.7 %all-to-all-start = ((bf16[32,6,3584]{2,1,0:T(8,128)(2,1)}), bf16[32,6,3584]{2,1,0:T(8,128)(2,1)S(1)}, u32[]{:S(2)}, u32[]{:S(2)}) async-start(bf16[32,6,3584]{2,1,0:T(8,128)(2,1)} %reshape.224), calls=%async_computation | async-start | bytes 3670016 | tf_op jit(solution)/shard_map/all_to_all | solution.py:57
  37.4 521.7 %all-gather.3.cloned.1.call-start = ((), (), s32[]{:S(2)}) async-start(), calls=%async_computation.4 | async-start | bytes 24772608 | tf_op jit(solution)/shard_map/all_gather | solution.py:71
  41.2 93.2 %copy-start = (bf16[1,3584,128]{2,1,0:T(8,128)(2,1)S(1)}, bf16[1,3584,128]{2,1,0:T(8,128)(2,1)}, u32[]{:S(2)}) copy-start(bf16[1,3584,128]{2,1,0:T(8,128)(2,1)} %param.14) | copy-start | bytes 2752516
  41.2 96.6 %copy-start.2 = (bf16[128,8]{0,1:T(8,128)(2,1)S(1)}, bf16[128,8]{0,1:T(8,128)(2,1)}, u32[]{:S(2)}) copy-start(bf16[128,8]{0,1:T(8,128)(2,1)} %param.11) | copy-start | bytes 6148
  44.7 101.6 %copy-start.3 = (s32[16]{0:T(128)S(1)}, s32[16]{0:T(128)}, u32[]{:S(2)}) copy-start(s32[16]{0:T(128)} %param.12) | copy-start | bytes 196
  134.4 495.3 %collective-permute-start.1 = (bf16[1,3584,128]{2,1,0:T(8,128)(2,1)S(1)}, bf16[1,3584,128]{2,1,0:T(8,128)(2,1)S(1)}, u32[]{:S(2)}, u32[]{:S(2)}) collective-permute-start(bf16[1,3584,128]{2,1,0:T(8,128)(2,1)S(1)} %copy-done), channel_id=1, source_target_pairs={{0,16},{16,0},{1,17},{17,1},{2,18},{18,2},{3,19},{19,3},{4,20},{20... | collective-permute-start | bytes 2752520 | tf_op jit(solution)/shard_map/ppermute | solution.py:16
  135.4 502.4 %collective-permute-start.2 = (bf16[1,3584,128]{2,1,0:T(8,128)(2,1)}, bf16[1,3584,128]{2,1,0:T(8,128)(2,1)}, u32[]{:S(2)}, u32[]{:S(2)}) collective-permute-start(bf16[1,3584,128]{2,1,0:T(8,128)(2,1)} %param.13), channel_id=1, source_target_pairs={{0,16},{16,0},{1,17},{17,1},{2,18},{18,2},{3,19},{19,3},{4,20},{20... | collective-permute-start | bytes 2752520 | tf_op jit(solution)/shard_map/ppermute | solution.py:16
  136.9 509.2 %collective-permute-start = (bf16[1,128,3584]{2,1,0:T(8,128)(2,1)}, bf16[1,128,3584]{2,1,0:T(8,128)(2,1)}, u32[]{:S(2)}, u32[]{:S(2)}) collective-permute-start(bf16[1,128,3584]{2,1,0:T(8,128)(2,1)} %param.15), channel_id=1, source_target_pairs={{0,16},{16,0},{1,17},{17,1},{2,18},{18,2},{3,19},{19,3},{4,20},{20... | collective-permute-start | bytes 2752520 | tf_op jit(solution)/shard_map/ppermute | solution.py:16
  140.4 295.0 %all-to-all-start.2 = ((bf16[32,1,6]{2,1,0:T(2,128)(2,1)}), bf16[32,1,6]{2,1,0:T(2,128)(2,1)S(1)}, u32[]{:S(2)}, u32[]{:S(2)}) async-start(bf16[32,1,6]{2,1,0:T(2,128)(2,1)} %all_to_all.27), calls=%async_computation.2 | async-start | bytes 32768 | tf_op jit(solution)/shard_map/all_to_all | solution.py:59
  629.8 16.3 %slice-start.3 = ((s8[11010048]{0:T(1024)(128)(4,1)}), s8[4194304]{0:T(1024)(128)(4,1)S(1)}, s32[]{:S(2)}) async-start(s8[11010048]{0:T(1024)(128)(4,1)} %bitcast.45), calls=%async_computation.8 | async-start | bytes 8388608
  629.8 16.3 %slice-start.4 = ((s8[11010048]{0:T(1024)(128)(4,1)}), s8[4194304]{0:T(1024)(128)(4,1)S(1)}, s32[]{:S(2)}) async-start(s8[11010048]{0:T(1024)(128)(4,1)} %bitcast.45), calls=%async_computation.9 | async-start | bytes 8388608
  637.8 8.3 %slice-start.5 = ((s8[11010048]{0:T(1024)(128)(4,1)}), s8[2621440]{0:T(1024)(128)(4,1)S(1)}, s32[]{:S(2)}) async-start(s8[11010048]{0:T(1024)(128)(4,1)} %bitcast.45), calls=%async_computation.10 | async-start | bytes 5242880
  637.8 14.0 %slice-start = ((s8[11010048]{0:T(1024)(128)(4,1)}), s8[4194304]{0:T(1024)(128)(4,1)S(1)}, s32[]{:S(2)}) async-start(s8[11010048]{0:T(1024)(128)(4,1)} %bitcast.43), calls=%async_computation.5 | async-start | bytes 8388608
  637.8 14.0 %slice-start.1 = ((s8[11010048]{0:T(1024)(128)(4,1)}), s8[2621440]{0:T(1024)(128)(4,1)S(1)}, s32[]{:S(2)}) async-start(s8[11010048]{0:T(1024)(128)(4,1)} %bitcast.43), calls=%async_computation.6 | async-start | bytes 5242880
  646.1 5.8 slice-start.2
  655.9 97.2 %copy-start.4 = (bf16[1536,128]{0,1:T(8,128)(2,1)S(1)}, bf16[1536,128]{0,1:T(8,128)(2,1)}, u32[]{:S(2)}) copy-start(bf16[1536,128]{0,1:T(8,128)(2,1)} %get-tuple-element.23) | copy-start | bytes 1179652
  660.2 108.5 %copy-start.1 = (s32[128,8]{0,1:T(8,128)S(1)}, s32[128,8]{0,1:T(8,128)}, u32[]{:S(2)}) copy-start(s32[128,8]{0,1:T(8,128)} %param.10) | copy-start | bytes 12292
  705.7 54.7 %all-to-all-start.3 = ((f32[32,1,6]{2,1,0:T(1,128)}), f32[32,1,6]{2,1,0:T(1,128)S(1)}, u32[]{:S(2)}, u32[]{:S(2)}) async-start(f32[32,1,6]{2,1,0:T(1,128)} %bitcast.11), calls=%async_computation.3 | async-start | bytes 32768 | tf_op jit(solution)/shard_map/all_to_all | solution.py:100
Sparse Core Ops, SparseCore 0:
  134.5 300.4 all-gather.2
